TPU v7x, 32 devices: a whole 2x2x4 slice. The times are simulated.
32 devices in a mesh: feat: 8 (over z, y), pair: 4 (over x, core).
Axes of the slice: x: 2, y: 2, z: 4, core: 2. Of those that a mesh axis runs over, the one named last changes fastest.
Arguments:
- in_factors: bfloat16 [512, 2, 512, 256], P(('feat', 'pair')), may hold values from -6 to 6
- out_factors: bfloat16 [512, 2, 512, 256], P(('feat', 'pair')), may hold values from -0.26367188 to 0.26367188
- token_counts: int32 [512, 2], P(('feat', 'pair')), may hold values from 1 to 512, as said below
- slot_pair: int32 [4, 128], P('pair'), may hold values from 0 to 127, each once within a row
- factor_panels: float32 [65536, 1536], P('feat'), as said below
Outputs:
- reduced: float32 [512, 65536], P('pair', 'feat')
Inputs may be any that keep to these rules, and one draw needn't show every extreme that they name: `token_counts`: column 0 counts the chosen response's tokens, column 1 the rejected one's; positions at or beyond the count are padding. `slot_pair`: each row is a permutation of 0 to 127. `factor_panels`: entries above the diagonal in the unknowns' order are zero: rows of panel j hold zeros in the columns of panels after j, and D_k has a positive diagonal.
All inputs are finite; a program needn't handle non-finite values.
Results may differ from a plain program's by a relative error of at most 0.0003.
Values sent between devices are 32-bit elements; how exact they have to be, the bound alone decides.
A program may use at most 128 MiB of HBM per device.

v0:
```python
import jax
import jax.numpy as jnp
from jax import lax
from jax.sharding import PartitionSpec as P

PANEL = 512
PANELS = 3


def spread(value, axis, source):
    kept = jnp.where(lax.axis_index(axis) == source, value, 0).astype(value.dtype)
    return lax.psum(kept, axis)


def panel_product(solved, panel_cols):
    return lax.dot_general(
        solved,
        panel_cols,
        (((1,), (1,)), ((), ())),
        precision=lax.Precision.HIGHEST,
        preferred_element_type=jnp.float32,
    )


def per_device(in_factors, out_factors, token_counts, slot_pair, factor_panels):
    slot_count, side_count, token_depth, proj_rank = in_factors.shape
    n_pair = lax.axis_size("pair")
    n_feat = lax.axis_size("feat")
    per_group = slot_count // n_pair
    row_count = factor_panels.shape[0]
    feat_index = lax.axis_index("feat")
    positions = lax.broadcasted_iota(jnp.int32, (slot_count, side_count, token_depth), 2)
    side_index = lax.broadcasted_iota(jnp.int32, (slot_count, side_count, token_depth), 1)
    weights = jnp.where(
        positions < token_counts[:, :, None], jnp.where(side_index == 0, 1.0, -1.0), 0.0
    ).astype(jnp.bfloat16)
    signed = out_factors * weights[..., None]
    gradients = jnp.einsum("ksti,kstj->kij", signed, in_factors, preferred_element_type=jnp.float32)
    gradients = gradients.reshape(n_pair, per_group, n_feat, row_count)
    group_pairs = slot_pair[0]
    pair_total = n_pair * n_feat * per_group
    outgoing = gradients.transpose(2, 0, 1, 3).reshape(n_feat * n_pair, per_group, row_count)
    received = lax.all_to_all(
        outgoing, ("feat", "pair"), split_axis=0, concat_axis=1, tiled=True
    ).reshape(pair_total, row_count)
    pair_rows = lax.broadcasted_iota(jnp.int32, (pair_total, pair_total), 0)
    placement = (pair_rows == group_pairs[None, :]).astype(jnp.float32)
    right_side = jnp.dot(
        placement, received, precision=lax.Precision.HIGHEST, preferred_element_type=jnp.float32
    )
    identity = jnp.eye(PANEL, dtype=jnp.float32)

    def solve_panel(k, current):
        diagonal = jnp.where(
            feat_index == k, factor_panels[:PANEL, k * PANEL : (k + 1) * PANEL], identity
        )
        solved = jax.scipy.linalg.solve_triangular(diagonal, current[:, :PANEL].T, lower=True).T
        return spread(solved, "feat", k)

    solved = solve_panel(0, right_side)
    for k in range(PANELS):
        panel_cols = factor_panels[:, k * PANEL : (k + 1) * PANEL]
        head_rows = right_side[:, :PANEL] - panel_product(solved, panel_cols[:PANEL])
        head_rows = jnp.where(feat_index == k, solved, head_rows)
        following = solved
        if k + 1 < PANELS:
            following = solve_panel(k + 1, head_rows)
        tail_rows = right_side[:, PANEL:] - panel_product(solved, panel_cols[PANEL:])
        right_side = jnp.concatenate([head_rows, tail_rows], axis=1)
        solved = following
    return right_side


def solution(mesh):
    return jax.shard_map(
        per_device,
        mesh=mesh,
        in_specs=(
            P(("feat", "pair"), None, None, None),
            P(("feat", "pair"), None, None, None),
            P(("feat", "pair"), None),
            P("pair", None),
            P("feat", None),
        ),
        out_specs=P("pair", "feat"),
        check_vma=False,
    )
```

profile of v0, /device:TPU:0, one launch (start us, length us, event | category | flops | bytes accessed | tf_op | source)
XLA Modules:
  0.0 420.1 jit_solution(17209154780739720358)
XLA Ops:
  6.5 0.8 copy.20
  7.4 9.8 %fusion.18 = f32[16,256,256]{2,1,0:T(8,128)} fusion(bf16[16,2,512,256]{3,2,1,0:T(8,128)(2,1)} %param.7, bf16[16,2,512,256]{3,2,1,0:T(8,128)(2,1)} %param.8, bf16[16,2,512]{2,1,0:T(2,128)(2,1)S(1)} %fusion.63), kind=kOutput, calls=%fused_computation.19 | convolution fusion | flops 2151677952 | bytes 21004288 | tf_op jit(solution)/shard_map/ksti,kstj->kij/dot_general | solution.py:38
  17.3 5.0 %reshape.28 = f32[4,4,8,8192]{3,2,1,0:T(8,128)} reshape(f32[16,256,256]{2,1,0:T(8,128)} %fusion.18) | data formatting | bytes 8388608 | tf_op jit(solution)/shard_map/reshape | solution.py:39
  22.2 6.9 %copy.22 = f32[4,4,8,8192]{3,1,0,2:T(4,128)} copy(f32[4,4,8,8192]{3,2,1,0:T(8,128)} %reshape.28) | data formatting | bytes 8388608 | tf_op jit(solution)/shard_map/reshape | solution.py:39
  29.1 7.5 %all-to-all-start = ((f32[32,4,8192]{2,1,0:T(4,128)}), f32[32,4,8192]{2,1,0:T(4,128)}, u32[]{:S(2)}, u32[]{:S(2)}) async-start(f32[32,4,8192]{2,1,0:T(4,128)} %bitcast.103), calls=%async_computation | async-start | bytes 8388608 | tf_op jit(solution)/shard_map/all_to_all | solution.py:43
  36.6 0.4 all-reduce.4.cloned.1.call-start
  37.0 2.3 fusion.24
  39.3 8.4 %while.6 = (s32[]{:T(128)}, f32[512,512]{1,0:T(8,128)S(1)}, s32[4,2]{0,1:T(2,128)S(1)}, f32[4,128,128]{2,1,0:T(8,128)S(1)}, s32[]{:T(128)}) while((s32[]{:T(128)}, f32[512,512]{1,0:T(8,128)S(1)}, s32[4,2]{0,1:T(2,128)S(1)}, f32[4,128,128]{2,1,0:T(8,128)S(1)}, s32[]{:T(128)}) %tuple.51), condition=%wide.while_cond, body=%wide.while_body.sunk | while | flops 2 | bytes 131189 | solution.py:57
  39.4 0.6 fusion.116
  40.0 1.4 bitcast_dynamic-update-slice_fusion.6
  41.5 0.6 fusion.116
  42.1 1.4 bitcast_dynamic-update-slice_fusion.6
  43.6 0.6 fusion.116
  44.2 1.4 bitcast_dynamic-update-slice_fusion.6
  45.7 0.6 fusion.116
  46.3 1.4 bitcast_dynamic-update-slice_fusion.6
  47.7 0.7 copy-done.4
  48.4 40.1 %custom-call.5 = f32[4,128,128]{1,2,0:T(8,128)S(1)} custom-call(f32[4,128,128]{2,1,0:T(8,128)} %copy-done.4), custom_call_target="InvertDiagBlocksLowerTriangular" | custom-call | tf_op jit(solution)/shard_map/jit(_solve_triangular)/triangular_solve | solution.py:57
  88.6 0.8 broadcast.62.clone.1
  89.3 9.7 %while.7 = (s32[]{:T(128)}, f32[512,512]{1,0:T(8,128)S(1)}, s32[4,2]{0,1:T(2,128)S(1)}, f32[4,128,128]{2,1,0:T(8,128)}, s32[]{:T(128)}) while((s32[]{:T(128)}, f32[512,512]{1,0:T(8,128)S(1)}, s32[4,2]{0,1:T(2,128)S(1)}, f32[4,128,128]{2,1,0:T(8,128)}, s32[]{:T(128)}) %tuple.66), condition=%wide.while_cond.clone, body=%wide.while_body.clone.sunk | while | flops 2 | bytes 132205 | solution.py:57
  89.4 0.5 fusion.117
  89.9 1.8 bitcast_dynamic-update-slice_fusion.7
  91.8 0.5 fusion.117
  92.3 1.8 bitcast_dynamic-update-slice_fusion.7
  94.3 0.5 fusion.117
  94.8 1.8 bitcast_dynamic-update-slice_fusion.7
  96.7 0.5 fusion.117
  97.2 1.8 bitcast_dynamic-update-slice_fusion.7
  99.0 31.2 %all-to-all-done = f32[32,4,8192]{2,1,0:T(4,128)} async-done(((f32[32,4,8192]{2,1,0:T(4,128)}), f32[32,4,8192]{2,1,0:T(4,128)}, u32[]{:S(2)}, u32[]{:S(2)}) %all-to-all-start) | async-done | bytes 4194336 | tf_op jit(solution)/shard_map/all_to_all | solution.py:43
  130.3 5.3 %reshape.30 = f32[128,8192]{1,0:T(8,128)} reshape(f32[32,4,8192]{2,1,0:T(4,128)} %all-to-all-done) | data formatting | bytes 8388608 | tf_op jit(solution)/shard_map/reshape | solution.py:45
  135.5 4.5 %fusion.82 = f32[128,8192]{1,0:T(8,128)S(1)} fusion(f32[128,8192]{1,0:T(8,128)} %reshape.30, s32[128]{0:T(128)S(1)} %bitcast.112), kind=kOutput, calls=%fused_computation.116 | convolution fusion | flops 1610629120 | bytes 8389120 | tf_op jit(solution)/shard_map/dot_general | solution.py:48
  140.1 2.0 copy-done
  143.0 0.4 convolution_subtract_fusion.7
  143.4 1.1 fusion.77
  144.5 0.5 convolution_subtract_fusion.11
  145.3 1.1 fusion.76
  146.4 0.7 fusion.30
  147.2 0.6 all-reduce.6.cloned.1.call-start
  147.8 7.8 %while.8 = (s32[]{:T(128)}, f32[512,512]{1,0:T(8,128)S(1)}, s32[4,2]{0,1:T(2,128)S(1)}, f32[4,128,128]{2,1,0:T(8,128)S(1)}, s32[]{:T(128)}) while((s32[]{:T(128)}, f32[512,512]{1,0:T(8,128)S(1)}, s32[4,2]{0,1:T(2,128)S(1)}, f32[4,128,128]{2,1,0:T(8,128)S(1)}, s32[]{:T(128)}) %tuple.67), condition=%wide.while_cond.clone.1, body=%wide.while_body.clone.1.sunk | while | flops 2 | bytes 131189 | solution.py:57
  147.9 0.6 fusion.118
  148.5 1.3 bitcast_dynamic-update-slice_fusion.8
  149.9 0.6 fusion.118
  150.4 1.3 bitcast_dynamic-update-slice_fusion.8
  151.8 0.6 fusion.118
  152.4 1.3 bitcast_dynamic-update-slice_fusion.8
  153.8 0.6 fusion.118
  154.3 1.3 bitcast_dynamic-update-slice_fusion.8
  155.6 40.1 %custom-call.6 = f32[4,128,128]{1,2,0:T(8,128)S(1)} custom-call(f32[4,128,128]{2,1,0:T(8,128)} %get-tuple-element.27), custom_call_target="InvertDiagBlocksLowerTriangular" | custom-call | tf_op jit(solution)/shard_map/jit(_solve_triangular)/triangular_solve | solution.py:57
  195.8 39.3 %custom-call.7 = f32[4,128,128]{1,2,0:T(8,128)S(1)} custom-call(f32[4,128,128]{2,1,0:T(8,128)S(1)} %get-tuple-element.28), custom_call_target="InvertDiagBlocksLowerTriangular" | custom-call | tf_op jit(solution)/shard_map/jit(_solve_triangular)/triangular_solve | solution.py:57
  235.1 2.6 fusion.23
  238.6 0.4 convolution_subtract_fusion.5
  239.3 0.5 convolution_subtract_fusion.10
  240.3 0.7 fusion.31
  241.3 21.2 %fusion.6 = f32[128,7680]{1,0:T(8,128)} fusion(f32[128,512]{1,0:T(8,128)S(1)} %copy-done.1, f32[8192,1536]{1,0:T(8,128)} %param.11, f32[128,8192]{1,0:T(8,128)} %copy-done), kind=kOutput, calls=%fused_computation.12 | convolution fusion | flops 6040780800 | bytes 23855104 | tf_op jit(solution)/shard_map/dot_general | solution.py:16
  262.5 49.2 %all-reduce.6.cloned.1.call-done = f32[128,512]{1,0:T(8,128)} async-done(((f32[128,512]{1,0:T(8,128)}), f32[128,512]{1,0:T(8,128)}) %all-reduce.6.cloned.1.call-update) | async-done | bytes 262160 | tf_op jit(solution)/shard_map/psum | solution.py:12
  311.7 2.6 fusion.22
  315.2 0.4 convolution_subtract_fusion.3
  315.9 0.5 convolution_subtract_fusion.9
  316.9 0.7 fusion.32
  317.6 23.0 %fusion.9 = f32[128,7680]{1,0:T(8,128)} fusion(f32[128,7680]{1,0:T(8,128)} %fusion.6, f32[128,512]{1,0:T(8,128)S(1)} %copy-done.2, f32[8192,1536]{1,0:T(8,128)} %param.11), kind=kOutput, calls=%fused_computation.13 | convolution fusion | flops 6040780800 | bytes 23855104 | tf_op jit(solution)/shard_map/dot_general | solution.py:16
  340.6 47.4 %all-reduce.8.cloned.1.call-done = f32[128,512]{1,0:T(8,128)} async-done(((f32[128,512]{1,0:T(8,128)}), f32[128,512]{1,0:T(8,128)}) %all-reduce.8.cloned.1.call-update) | async-done | bytes 262160 | tf_op jit(solution)/shard_map/psum | solution.py:12
  388.0 2.5 fusion.21
  390.5 20.4 %fusion.12 = f32[128,7680]{1,0:T(8,128)S(1)} fusion(f32[128,7680]{1,0:T(8,128)} %fusion.9, f32[128,512]{1,0:T(8,128)} %all-reduce.8.cloned.1.call-done, f32[8192,1536]{1,0:T(8,128)} %param.11), kind=kOutput, calls=%fused_computation.14 | convolution fusion | flops 6040780800 | bytes 23855104 | tf_op jit(solution)/shard_map/dot_general | solution.py:16
  411.0 2.3 pad_maximum_fusion
  (56 shorter events, 5.7 us)
Async XLA Ops:
  29.1 101.2 %all-to-all-start = ((f32[32,4,8192]{2,1,0:T(4,128)}), f32[32,4,8192]{2,1,0:T(4,128)}, u32[]{:S(2)}, u32[]{:S(2)}) async-start(f32[32,4,8192]{2,1,0:T(4,128)} %bitcast.103), calls=%async_computation | async-start | bytes 8388608 | tf_op jit(solution)/shard_map/all_to_all | solution.py:43
  36.6 198.5 %all-reduce.4.cloned.1.call-start = ((), (), s32[]{:S(2)}) async-start(), calls=%async_computation.1 | async-start | bytes 524288 | tf_op jit(solution)/shard_map/psum | solution.py:12
  47.7 0.7 copy-start.4
  88.6 54.2 %copy-start.3 = (f32[4,128,128]{1,2,0:T(8,128)}, f32[4,128,128]{1,2,0:T(8,128)S(1)}, u32[]{:S(2)}) copy-start(f32[4,128,128]{1,2,0:T(8,128)S(1)} %custom-call.5) | copy-start | bytes 786436
  99.0 36.5 %copy-start.5 = (s32[1,128]{1,0:T(1,128)S(1)}, s32[1,128]{1,0:T(1,128)}, u32[]{:S(2)}) copy-start(s32[1,128]{1,0:T(1,128)} %param.10) | copy-start | bytes 1540
  140.1 2.0 copy-start
  147.2 164.6 %all-reduce.6.cloned.1.call-start = ((), (), s32[]{:S(2)}) async-start(), calls=%async_computation.2 | async-start | bytes 524288 | tf_op jit(solution)/shard_map/psum | solution.py:12
  235.1 6.2 %copy-start.1 = (f32[128,512]{1,0:T(8,128)S(1)}, f32[128,512]{1,0:T(8,128)}, u32[]{:S(2)}) copy-start(f32[128,512]{1,0:T(8,128)} %all-reduce.4.cloned.1.call-done) | copy-start | bytes 786436
  241.1 146.9 %all-reduce.8.cloned.1.call-start = ((), (), s32[]{:S(2)}) async-start(), calls=%async_computation.3 | async-start | bytes 524288 | tf_op jit(solution)/shard_map/psum | solution.py:12
  311.7 5.9 %copy-start.2 = (f32[128,512]{1,0:T(8,128)S(1)}, f32[128,512]{1,0:T(8,128)}, u32[]{:S(2)}) copy-start(f32[128,512]{1,0:T(8,128)} %all-reduce.6.cloned.1.call-done) | copy-start | bytes 786436
Sparse Core Ops, SparseCore 0:
  147.3 71.4 all-reduce.3
  241.2 70.4 all-reduce.5
  317.8 70.1 all-reduce.7
where the time goes:
time: 425 us; the launch traced here: 420 us
  waiting for transfers between devices  128 us (30%)
  other arithmetic  126 us (30%)
  matrix products  95.1 us (22%)
  local copies, waits for them, and re-layouts  48 us (11%)
  between operations  13.8 us (3%)
  starting transfers between devices  8.67 us (2%)
    another operation x5, other arithmetic, solve_panel(): jax.scipy.linalg.solve_triangular(diagonal, current[:, :PANEL].T, lower=T...  122 us
    psum x3, waiting for transfers between devices, spread(): return lax.psum(kept, axis)  96.6 us
    dot_general x6, matrix products, panel_product(): lax.dot_general(solved, panel_cols, (((1,), (1,)), ((), ())), precision=l...  72.3 us
    all_to_all x1, waiting for transfers between devices, per_device(): lax.all_to_all(outgoing, ('feat', 'pair'), split_axis=0, concat_axis=1, t...  31.2 us
    another operation x49, local copies, waits for them, and re-layouts, solve_panel(): jax.scipy.linalg.solve_triangular(diagonal, current[:, :PANEL].T, lower=T...  27.4 us
    reshape x2, local copies, waits for them, and re-layouts, per_device(): gradients = gradients.reshape(n_pair, per_group, n_feat, row_count)  11.9 us
    dot_general x1, matrix products, per_device(): jnp.einsum('ksti,kstj->kij', signed, in_factors, preferred_element_type=j...  9.84 us
  transfers between devices with their start and end apart: 4, of which 3 were waited for; matrix products, arithmetic and copies ran while one was open for 46% of the time, Pallas kernels for 0%

commit v1 on v0

--- a/solution.py
+++ b/solution.py
@@ -9,7 +9,7 @@
 
 def spread(value, axis, source):
     kept = jnp.where(lax.axis_index(axis) == source, value, 0).astype(value.dtype)
-    return lax.psum(kept, axis)
+    return jnp.sum(lax.all_gather(kept, axis), axis=0)
 
 
 def panel_product(solved, panel_cols):

time: 425 us -> 356 us (0.84)
  waiting for transfers between devices: 128 us -> 49.2 us
  local copies, waits for them, and re-layouts: 48 us -> 53.6 us
    psum x3 -> x0, waiting for transfers between devices: 96.6 us -> none  [spread(): return lax.psum(kept, axis)]
    all_gather x0 -> x3, waiting for transfers between devices: none -> 10.3 us  [spread(): return jnp.sum(lax.all_gather(kept, axis), axis=0)]
    all_to_all x1, waiting for transfers between devices: 31.2 us -> 38.9 us  [per_device(): lax.all_to_all(outgoing, ('feat', 'pair'), split_axis=0, concat_axis=1, t...]
    unnamed x13 -> x8, local copies, waits for them, and re-layouts: 3.47 us -> 8.94 us
    another operation x49 -> x40, local copies, waits for them, and re-layouts: 27.4 us -> 27.2 us  [solve_panel(): jax.scipy.linalg.solve_triangular(diagonal, current[:, :PANEL].T, lower=T...]
  transfers between devices with their start and end apart: 4 -> 4, of which waited for: 3 -> 4; matrix products, arithmetic and copies ran while one was open for 46% -> 55% of each run, Pallas kernels for 0% -> 0%
where the time goes in v1:
time: 356 us; the launch traced here: 351 us
  other arithmetic  127 us (36%)
  matrix products  98 us (28%)
  local copies, waits for them, and re-layouts  53.6 us (15%)
  waiting for transfers between devices  49.2 us (14%)
  between operations  13.7 us (4%)
  starting transfers between devices  8.48 us (2%)
    another operation x5, other arithmetic, solve_panel(): jax.scipy.linalg.solve_triangular(diagonal, current[:, :PANEL].T, lower=T...  121 us
    dot_general x6, matrix products, panel_product(): lax.dot_general(solved, panel_cols, (((1,), (1,)), ((), ())), precision=l...  74 us
    all_to_all x1, waiting for transfers between devices, per_device(): lax.all_to_all(outgoing, ('feat', 'pair'), split_axis=0, concat_axis=1, t...  38.9 us
    another operation x40, local copies, waits for them, and re-layouts, solve_panel(): jax.scipy.linalg.solve_triangular(diagonal, current[:, :PANEL].T, lower=T...  27.2 us
    reshape x2, local copies, waits for them, and re-layouts, per_device(): gradients = gradients.reshape(n_pair, per_group, n_feat, row_count)  11.9 us
    all_gather x3, waiting for transfers between devices, spread(): return jnp.sum(lax.all_gather(kept, axis), axis=0)  10.3 us
    dot_general x1, matrix products, per_device(): jnp.einsum('ksti,kstj->kij', signed, in_factors, preferred_element_type=j...  9.84 us
    another operation x21, matrix products, solve_panel(): jax.scipy.linalg.solve_triangular(diagonal, current[:, :PANEL].T, lower=T...  9.6 us
  transfers between devices with their start and end apart: 4, of which 4 were waited for; matrix products, arithmetic and copies ran while one was open for 55% of the time, Pallas kernels for 0%

profile of v1, /device:TPU:0, one launch (start us, length us, event | category | flops | bytes accessed | tf_op | source)
XLA Modules:
  0.0 350.7 jit_solution(13696615634756668367)
XLA Ops:
  6.5 0.8 copy.11
  7.4 9.8 %fusion.18 = f32[16,256,256]{2,1,0:T(8,128)} fusion(bf16[16,2,512,256]{3,2,1,0:T(8,128)(2,1)} %param.7, bf16[16,2,512,256]{3,2,1,0:T(8,128)(2,1)} %param.8, bf16[16,2,512]{2,1,0:T(2,128)(2,1)S(1)} %fusion.63), kind=kOutput, calls=%fused_computation.19 | convolution fusion | flops 2151677952 | bytes 21004288 | tf_op jit(solution)/shard_map/ksti,kstj->kij/dot_general | solution.py:38
  17.3 5.0 %reshape.28 = f32[4,4,8,8192]{3,2,1,0:T(8,128)} reshape(f32[16,256,256]{2,1,0:T(8,128)} %fusion.18) | data formatting | bytes 8388608 | tf_op jit(solution)/shard_map/reshape | solution.py:39
  22.2 6.9 %copy.13 = f32[4,4,8,8192]{3,1,0,2:T(4,128)} copy(f32[4,4,8,8192]{3,2,1,0:T(8,128)} %reshape.28) | data formatting | bytes 8388608 | tf_op jit(solution)/shard_map/reshape | solution.py:39
  29.1 7.5 %all-to-all-start = ((f32[32,4,8192]{2,1,0:T(4,128)}), f32[32,4,8192]{2,1,0:T(4,128)}, u32[]{:S(2)}, u32[]{:S(2)}) async-start(f32[32,4,8192]{2,1,0:T(4,128)} %bitcast.118), calls=%async_computation | async-start | bytes 8388608 | tf_op jit(solution)/shard_map/all_to_all | solution.py:43
  36.6 0.6 all-gather.7.cloned.1.call-start
  37.2 3.3 fusion.24
  40.5 11.6 %while.6 = (s32[]{:T(128)}, f32[512,512]{1,0:T(8,128)}, s32[4,2]{0,1:T(2,128)S(1)}, f32[4,128,128]{2,1,0:T(8,128)S(1)}, s32[]{:T(128)}) while((s32[]{:T(128)}, f32[512,512]{1,0:T(8,128)}, s32[4,2]{0,1:T(2,128)S(1)}, f32[4,128,128]{2,1,0:T(8,128)S(1)}, s32[]{:T(128)}) %tuple.51), condition=%wide.while_cond, body=%wide.while_body.sunk | while | flops 2 | bytes 131189 | solution.py:57
  40.6 0.5 fusion.116
  41.1 2.3 bitcast_dynamic-update-slice_fusion.6
  43.5 0.5 fusion.116
  44.0 2.3 bitcast_dynamic-update-slice_fusion.6
  46.4 0.5 fusion.116
  46.9 2.3 bitcast_dynamic-update-slice_fusion.6
  49.3 0.5 fusion.116
  49.8 2.2 bitcast_dynamic-update-slice_fusion.6
  52.0 39.3 %custom-call.5 = f32[4,128,128]{1,2,0:T(8,128)S(1)} custom-call(f32[4,128,128]{2,1,0:T(8,128)S(1)} %get-tuple-element.26), custom_call_target="InvertDiagBlocksLowerTriangular" | custom-call | tf_op jit(solution)/shard_map/jit(_solve_triangular)/triangular_solve | solution.py:57
  91.4 38.9 %all-to-all-done = f32[32,4,8192]{2,1,0:T(4,128)} async-done(((f32[32,4,8192]{2,1,0:T(4,128)}), f32[32,4,8192]{2,1,0:T(4,128)}, u32[]{:S(2)}, u32[]{:S(2)}) %all-to-all-start) | async-done | bytes 4194336 | tf_op jit(solution)/shard_map/all_to_all | solution.py:43
  130.3 5.3 %reshape.30 = f32[128,8192]{1,0:T(8,128)} reshape(f32[32,4,8192]{2,1,0:T(4,128)} %all-to-all-done) | data formatting | bytes 8388608 | tf_op jit(solution)/shard_map/reshape | solution.py:45
  135.5 4.5 %fusion.82 = f32[128,8192]{1,0:T(8,128)S(1)} fusion(f32[128,8192]{1,0:T(8,128)} %reshape.30, s32[128]{0:T(128)S(1)} %bitcast.130), kind=kOutput, calls=%fused_computation.119 | convolution fusion | flops 1610629120 | bytes 8389120 | tf_op jit(solution)/shard_map/dot_general | solution.py:48
  140.1 2.0 copy-done
  142.4 1.1 convolution_subtract_fusion.8
  143.8 1.3 convolution_subtract_fusion.7
  145.4 1.4 convolution_subtract_fusion.11
  147.2 0.7 fusion.30
  148.1 7.9 %while.7 = (s32[]{:T(128)}, f32[512,512]{1,0:T(8,128)S(1)}, s32[4,2]{0,1:T(2,128)S(1)}, f32[4,128,128]{2,1,0:T(8,128)S(1)}, s32[]{:T(128)}) while((s32[]{:T(128)}, f32[512,512]{1,0:T(8,128)S(1)}, s32[4,2]{0,1:T(2,128)S(1)}, f32[4,128,128]{2,1,0:T(8,128)S(1)}, s32[]{:T(128)}) %tuple.66), condition=%wide.while_cond.clone, body=%wide.while_body.clone.sunk | while | flops 2 | bytes 131189 | solution.py:57
  148.2 0.6 fusion.117
  148.8 1.3 bitcast_dynamic-update-slice_fusion.7
  150.2 0.6 fusion.117
  150.8 1.3 bitcast_dynamic-update-slice_fusion.7
  152.2 0.6 fusion.117
  152.7 1.3 bitcast_dynamic-update-slice_fusion.7
  154.2 0.6 fusion.117
  154.7 1.3 bitcast_dynamic-update-slice_fusion.7
  156.1 39.3 %custom-call.6 = f32[4,128,128]{1,2,0:T(8,128)S(1)} custom-call(f32[4,128,128]{2,1,0:T(8,128)S(1)} %get-tuple-element.27), custom_call_target="InvertDiagBlocksLowerTriangular" | custom-call | tf_op jit(solution)/shard_map/jit(_solve_triangular)/triangular_solve | solution.py:57
  195.4 2.6 all-gather.7.cloned.1.call-done
  198.0 2.1 copy.37
  200.1 0.6 bitcast_reduce_fusion.2
  200.8 2.5 fusion.23
  205.6 0.7 fusion.31
  206.7 7.9 %while.8 = (s32[]{:T(128)}, f32[512,512]{1,0:T(8,128)S(1)}, s32[4,2]{0,1:T(2,128)S(1)}, f32[4,128,128]{2,1,0:T(8,128)S(1)}, s32[]{:T(128)}) while((s32[]{:T(128)}, f32[512,512]{1,0:T(8,128)S(1)}, s32[4,2]{0,1:T(2,128)S(1)}, f32[4,128,128]{2,1,0:T(8,128)S(1)}, s32[]{:T(128)}) %tuple.67), condition=%wide.while_cond.clone.1, body=%wide.while_body.clone.1.sunk | while | flops 2 | bytes 131189 | solution.py:57
  206.8 0.6 fusion.118
  207.3 1.3 bitcast_dynamic-update-slice_fusion.8
  208.7 0.6 fusion.118
  209.3 1.3 bitcast_dynamic-update-slice_fusion.8
  210.7 0.6 fusion.118
  211.3 1.3 bitcast_dynamic-update-slice_fusion.8
  212.7 0.6 fusion.118
  213.2 1.3 bitcast_dynamic-update-slice_fusion.8
  214.6 39.3 %custom-call.7 = f32[4,128,128]{1,2,0:T(8,128)S(1)} custom-call(f32[4,128,128]{2,1,0:T(8,128)S(1)} %get-tuple-element.28), custom_call_target="InvertDiagBlocksLowerTriangular" | custom-call | tf_op jit(solution)/shard_map/jit(_solve_triangular)/triangular_solve | solution.py:57
  253.9 3.5 all-gather.9.cloned.1.call-done
  257.4 2.1 copy.38
  259.4 0.6 bitcast_reduce_fusion.1
  260.1 2.5 fusion.22
  264.2 0.5 convolution_subtract_fusion.9
  265.0 0.7 fusion.32
  265.7 20.7 %fusion.6 = f32[128,7680]{1,0:T(8,128)S(1)} fusion(f32[128,512]{0,1:T(8,128)S(1)} %bitcast_reduce_fusion.2, f32[8192,1536]{1,0:T(8,128)} %param.11, f32[128,8192]{1,0:T(8,128)} %copy-done), kind=kOutput, calls=%fused_computation.12 | convolution fusion | flops 6040780800 | bytes 23855104 | tf_op jit(solution)/shard_map/dot_general | solution.py:16
  286.4 23.1 %fusion.9 = f32[128,7680]{1,0:T(8,128)} fusion(f32[128,7680]{1,0:T(8,128)S(1)} %fusion.6, f32[128,512]{0,1:T(8,128)S(1)} %bitcast_reduce_fusion.1, f32[8192,1536]{1,0:T(8,128)} %param.11), kind=kOutput, calls=%fused_computation.13 | convolution fusion | flops 6040780800 | bytes 23855104 | tf_op jit(solution)/shard_map/dot_general | solution.py:16
  309.5 4.2 %all-gather.11.cloned.1.call-done = f32[1024,512]{0,1:T(8,128)} async-done(((f32[128,512]{0,1:T(8,128)}), f32[1024,512]{0,1:T(8,128)}) %all-gather.11.cloned.1.call-update) | async-done | bytes 2097168 | tf_op jit(solution)/shard_map/all_gather | solution.py:12
  313.7 2.1 copy.39
  315.8 0.6 bitcast_reduce_fusion
  316.5 22.7 %fusion.12 = f32[128,7680]{1,0:T(8,128)S(1)} fusion(f32[128,7680]{1,0:T(8,128)} %fusion.9, f32[128,512]{0,1:T(8,128)S(1)} %bitcast_reduce_fusion, f32[8192,1536]{1,0:T(8,128)} %param.11), kind=kOutput, calls=%fused_computation.14 | convolution fusion | flops 6040780800 | bytes 23855104 | tf_op jit(solution)/shard_map/dot_general | solution.py:16
  339.2 2.5 fusion.21
  341.7 2.3 pad_maximum_fusion
  (48 shorter events, 7.2 us)
Async XLA Ops:
  29.1 101.2 %all-to-all-start = ((f32[32,4,8192]{2,1,0:T(4,128)}), f32[32,4,8192]{2,1,0:T(4,128)}, u32[]{:S(2)}, u32[]{:S(2)}) async-start(f32[32,4,8192]{2,1,0:T(4,128)} %bitcast.118), calls=%async_computation | async-start | bytes 8388608 | tf_op jit(solution)/shard_map/all_to_all | solution.py:43
  36.6 161.4 %all-gather.7.cloned.1.call-start = ((), (), s32[]{:S(2)}) async-start(), calls=%async_computation.1 | async-start | bytes 2359296 | tf_op jit(solution)/shard_map/all_gather | solution.py:12
  91.4 44.2 %copy-start.1 = (s32[1,128]{1,0:T(1,128)S(1)}, s32[1,128]{1,0:T(1,128)}, u32[]{:S(2)}) copy-start(s32[1,128]{1,0:T(1,128)} %param.10) | copy-start | bytes 1540
  140.1 2.0 copy-start
  147.9 109.5 %all-gather.9.cloned.1.call-start = ((), (), s32[]{:S(2)}) async-start(), calls=%async_computation.2 | async-start | bytes 2359296 | tf_op jit(solution)/shard_map/all_gather | solution.py:12
  206.4 107.3 %all-gather.11.cloned.1.call-start = ((), (), s32[]{:S(2)}) async-start(), calls=%async_computation.3 | async-start | bytes 2359296 | tf_op jit(solution)/shard_map/all_gather | solution.py:12
Sparse Core Ops, SparseCore 0:
  148.0 49.9 all-gather.6
  206.5 50.8 all-gather.8
  265.8 47.8 all-gather.10
